TPU v7x, 32 devices: a whole 2x2x4 slice. The times are simulated.
32 devices in a mesh: depth: 4 (over y, x), tile: 8 (over z, core).
Axes of the slice: x: 2, y: 2, z: 4, core: 2. Of those that a mesh axis runs over, the one named last changes fastest.
Arguments:
- objects: float32 [4, 4096, 4096], P('depth', 'tile'), may hold values from -6 to 6
- transfer: bfloat16 [4, 2, 4096, 4096], P('depth', None, None, 'tile'), may hold values from -3 to 3
Outputs:
- sensor: float32 [4096, 4096], P(('depth', 'tile'))
All inputs are finite; a program needn't handle non-finite values.
Results may differ from a plain program's by a relative error of at most 0.0003.
Values sent between devices are 32-bit elements; how exact they have to be, the bound alone decides.
A program may use at most 128 MiB of HBM per device.

v0:
```python
import math

import jax
import jax.numpy as jnp
from jax import lax
from jax.sharding import PartitionSpec as P


def circle(count_rows, count_cols, modulus, direction):
    row_index = jnp.arange(count_rows, dtype=jnp.int32)[:, None]
    col_index = jnp.arange(count_cols, dtype=jnp.int32)[None, :]
    turn_count = (row_index * col_index % modulus).astype(jnp.float32)
    phase = direction * 2.0 * math.pi * turn_count / modulus
    return (jnp.cos(phase), jnp.sin(phase))


def blocked(real_part, imag_part):
    return jnp.stack([jnp.stack([real_part, imag_part]), jnp.stack([-imag_part, real_part])])


def contract(form, values, matrix):
    return jnp.einsum(
        form, values, matrix, precision=lax.Precision.HIGHEST, preferred_element_type=jnp.float32
    )


def transform(values, direction, layout, real_input=False, real_only=False):
    if layout == "col":
        length = values.shape[-2]
        batch_len = values.shape[-1]
    else:
        length = values.shape[-1]
        batch_len = values.shape[-2]
    outer_len = 2 ** ((length.bit_length() - 1) // 2)
    inner_len = length // outer_len
    outer_re, outer_im = circle(outer_len, outer_len, outer_len, direction)
    outer_mat = blocked(outer_re, outer_im)
    twist_re, twist_im = circle(outer_len, inner_len, length, direction)
    inner_re, inner_im = circle(inner_len, inner_len, inner_len, direction)
    inner_mat = blocked(inner_re, inner_im)
    if layout == "col":
        shape_in = (outer_len, inner_len, batch_len)
        form_one = ("abr", "kbr")
        form_two = ("kbr", "ckr")
        twist_re, twist_im = (twist_re[:, :, None], twist_im[:, :, None])
    elif layout == "rowT":
        shape_in = (batch_len, outer_len, inner_len)
        form_one = ("rab", "kbr")
        form_two = ("kbr", "ckr")
        twist_re, twist_im = (twist_re[:, :, None], twist_im[:, :, None])
    else:
        shape_in = (batch_len, outer_len, inner_len)
        form_one = ("rab", "rkb")
        form_two = ("rkb", "rck")
        twist_re, twist_im = (twist_re[None], twist_im[None])
    if real_input:
        middle = contract(
            form_one[0] + ",tak->t" + form_one[1], values.reshape(shape_in), outer_mat[0]
        )
    else:
        middle = contract(
            "s" + form_one[0] + ",stak->t" + form_one[1], values.reshape((2,) + shape_in), outer_mat
        )
    turned = jnp.stack(
        [middle[0] * twist_re - middle[1] * twist_im, middle[0] * twist_im + middle[1] * twist_re]
    )
    if layout == "row":
        shape_out = (batch_len, length)
    else:
        shape_out = (length, batch_len)
    form_full = "s" + form_two[0] + ",stbc->t" + form_two[1]
    if real_only:
        return contract(form_full, turned, inner_mat[:, :1])[0].reshape(shape_out)
    return contract(form_full, turned, inner_mat).reshape((2,) + shape_out)


def body(objects, transfer):
    tile_count = lax.axis_size("tile")
    full_rows = objects.shape[1] * tile_count
    norm_factor = 1.0 / (full_rows * objects.shape[2])
    row_spec = transform(objects[0], -1.0, "rowT", real_input=True)
    col_spec = lax.all_to_all(row_spec, "tile", split_axis=1, concat_axis=2, tiled=True)
    spectrum = transform(col_spec, -1.0, "rowT")
    response = transfer[0].astype(jnp.float32)
    products = jnp.stack(
        [
            spectrum[0] * response[0] - spectrum[1] * response[1],
            spectrum[0] * response[1] + spectrum[1] * response[0],
        ]
    )
    back_cols = transform(products, 1.0, "col")
    partial_rows = lax.psum_scatter(back_cols, "depth", scatter_dimension=1, tiled=True)
    band_data = lax.all_to_all(partial_rows, "tile", split_axis=1, concat_axis=2, tiled=True)
    final_rows = transform(band_data, 1.0, "row", real_only=True)
    return final_rows * norm_factor


def solution(mesh):
    in_specs = (P("depth", "tile", None), P("depth", None, None, "tile"))
    out_specs = P(("depth", "tile"), None)
    return jax.shard_map(body, mesh=mesh, in_specs=in_specs, out_specs=out_specs, check_vma=False)
```

profile of v0, /device:TPU:0, one launch (start us, length us, event | category | flops | bytes accessed | tf_op | source)
XLA Modules:
  0.0 1053.6 jit_solution(7974038136439149113)
XLA Ops:
  6.5 0.1 multiply_sine_fusion.2
  6.7 0.1 multiply_sine_fusion.1
  6.8 0.1 fusion.70
  7.0 9.0 copy.62
  16.0 25.0 %fusion.20 = f32[2,64,64,512]{3,1,2,0:T(8,128)S(1)} fusion(f32[512,64,64]{0,2,1:T(8,128)} %bitcast.149, f32[1,64,64]{1,2,0:T(8,128)S(1)} %get-tuple-element.21, f32[1,64,64]{1,2,0:T(8,128)S(1)} %get-tuple-element.22), kind=kOutput, calls=%fused_computation.36 | convolution fusion | flops 3221233664 | bytes 25198592 | tf_op jit(solution)/shard_map/rab,tak->tkbr/dot_general | solution.py:22
  41.1 6.8 multiply_subtract_fusion.2
  47.8 12.1 %pad_maximum_fusion = f32[2,64,64,512]{3,1,2,0:T(8,128)} fusion(f32[1,64,64,512]{3,1,2,0:T(8,128)} %get-tuple-element.12, f32[1,64,64,512]{3,1,2,0:T(8,128)} %get-tuple-element.11), kind=kLoop, calls=%fused_computation | loop fusion | flops 4194304 | bytes 33554432 | tf_op jit(solution)/shard_map/stack | solution.py:64
  60.0 33.0 %fusion.23 = f32[2,64,64,512]{3,1,2,0:T(8,128)} fusion(f32[2,64,64,512]{3,1,2,0:T(8,128)} %pad_maximum_fusion, f32[1,2,64,64]{2,3,1,0:T(8,128)S(1)} %get-tuple-element.20, f32[1,2,64,64]{2,3,1,0:T(8,128)S(1)} %get-tuple-element.19), kind=kOutput, calls=%fused_computation.37 | convolution fusion | flops 6442467328 | bytes 33619968 | tf_op jit(solution)/shard_map/skbr,stbc->tckr/dot_general | solution.py:22
  93.0 15.3 %copy.66 = f32[2,64,64,512]{3,2,1,0:T(8,128)S(1)} copy(f32[2,64,64,512]{3,1,2,0:T(8,128)} %fusion.23) | data formatting | bytes 33554432 | tf_op jit(solution)/shard_map/skbr,stbc->tckr/dot_general | solution.py:22
  108.2 32.2 %copy.67 = f32[2,4096,512]{2,0,1:T(2,128)} copy(f32[2,4096,512]{2,1,0:T(8,128)S(1)} %bitcast.146) | data formatting | bytes 33554432 | tf_op jit(solution)/shard_map/reshape | solution.py:74
  140.5 6.4 all-to-all-start
  146.8 0.0 reduce-scatter.2.cloned.1.call-start
  146.9 11.5 %convert_element_type.113 = f32[1,2,4096,512]{3,2,1,0:T(8,128)} convert(bf16[1,2,4096,512]{3,2,1,0:T(8,128)(2,1)} %param.3) | non-fusion elementwise | flops 4194304 | bytes 25165824 | tf_op jit(solution)/shard_map/convert_element_type | solution.py:84
  158.4 0.1 fusion.69
  158.6 0.1 multiply_sine_fusion.3
  158.7 0.1 multiply_sine_fusion
  158.9 351.8 %all-to-all-done = f32[2,4096,512]{2,0,1:T(2,128)} async-done(((f32[2,4096,512]{2,0,1:T(2,128)}), f32[2,4096,512]{2,0,1:T(2,128)}, u32[]{:S(2)}, u32[]{:S(2)}) %all-to-all-start) | async-done | bytes 16777248 | tf_op jit(solution)/shard_map/all_to_all | solution.py:82
  510.7 14.1 %copy.68 = f32[2,4096,512]{2,1,0:T(8,128)} copy(f32[2,4096,512]{2,0,1:T(2,128)} %all-to-all-done) | data formatting | bytes 33554432 | tf_op jit(solution)/shard_map/all_to_all | solution.py:82
  524.8 17.3 %copy.69 = f32[2,512,8,512]{1,3,2,0:T(8,128)} copy(f32[2,512,8,512]{3,1,2,0:T(8,128)} %bitcast.147) | data formatting | bytes 33554432 | tf_op jit(solution)/shard_map/all_to_all | solution.py:82
  542.1 32.8 %fusion.26 = f32[2,64,64,512]{3,1,2,0:T(8,128)} fusion(f32[2,512,64,64]{1,3,2,0:T(8,128)} %bitcast.148, f32[1,2,64,64]{2,3,1,0:T(8,128)S(1)} %get-tuple-element.20, f32[1,2,64,64]{2,3,1,0:T(8,128)S(1)} %get-tuple-element.19), kind=kOutput, calls=%fused_computation.38 | convolution fusion | flops 6442467328 | bytes 33619968 | tf_op jit(solution)/shard_map/srab,stak->tkbr/dot_general | solution.py:22
  575.0 6.9 multiply_subtract_fusion.1
  581.9 6.2 pad_maximum_fusion.1
  588.1 33.0 %fusion.29 = f32[2,64,64,512]{3,1,2,0:T(8,128)} fusion(f32[2,64,64,512]{3,1,2,0:T(8,128)} %pad_maximum_fusion.1, f32[1,2,64,64]{2,3,1,0:T(8,128)S(1)} %get-tuple-element.20, f32[1,2,64,64]{2,3,1,0:T(8,128)S(1)} %get-tuple-element.19), kind=kOutput, calls=%fused_computation.39 | convolution fusion | flops 6442467328 | bytes 33619968 | tf_op jit(solution)/shard_map/skbr,stbc->tckr/dot_general | solution.py:22
  621.1 6.9 fusion.74
  628.0 8.1 copy.74
  636.1 8.1 copy.75
  644.2 19.4 %fusion.15 = (f32[1,4096,512]{2,1,0:T(8,128)}, f32[1,4096,512]{2,1,0:T(8,128)}) fusion(f32[1,64,64,512]{3,2,1,0:T(8,128)} %copy.75, f32[1,64,64,512]{3,2,1,0:T(8,128)} %copy.74, f32[1,2,4096,512]{3,2,1,0:T(8,128)} %convert_element_type.113), kind=kLoop, calls=%fused_computation.23 | loop fusion | flops 12582912 | bytes 50331648 | tf_op jit(solution)/shard_map/sub | solution.py:87
  663.6 0.0 copy-start
  663.6 8.4 copy.76
  672.0 0.0 copy-done
  672.0 8.1 copy.77
  680.0 19.1 %fusion.35 = f32[2,64,64,512]{3,1,2,0:T(8,128)} fusion(f32[1,64,64,512]{3,1,0,2:T(8,128)} %copy.77, f32[1,64,64,512]{3,1,0,2:T(8,128)S(1)} %copy.76, f32[1,2,64,64]{2,3,1,0:T(8,128)S(1)} %get-tuple-element.18, f32[1,2,64,64]{2,3,1,0:T(8,128)S(1)} %get-tuple-element.17), kind=kOutput, calls=%fused_computation.41 | convolution fusion | flops 6446661632 | bytes 33619968 | tf_op jit(solution)/shard_map/sabr,stak->tkbr/dot_general | solution.py:22
  699.2 6.9 multiply_subtract_fusion
  706.1 6.2 pad_maximum_fusion.2
  712.3 33.0 %fusion.32 = f32[2,64,64,512]{3,1,2,0:T(8,128)} fusion(f32[2,64,64,512]{3,1,2,0:T(8,128)} %pad_maximum_fusion.2, f32[1,2,64,64]{2,3,1,0:T(8,128)S(1)} %get-tuple-element.18, f32[1,2,64,64]{2,3,1,0:T(8,128)S(1)} %get-tuple-element.17), kind=kOutput, calls=%fused_computation.40 | convolution fusion | flops 6442467328 | bytes 33619968 | tf_op jit(solution)/shard_map/skbr,stbc->tckr/dot_general | solution.py:22
  745.3 17.7 %copy.81 = f32[2,64,64,512]{3,2,1,0:T(8,128)} copy(f32[2,64,64,512]{3,1,2,0:T(8,128)} %fusion.32) | data formatting | bytes 33554432 | tf_op jit(solution)/shard_map/skbr,stbc->tckr/dot_general | solution.py:22
  763.0 0.0 reduce-scatter.2.cloned.1.call-update
  763.0 153.4 %reduce-scatter.2.cloned.1.call-done = f32[2,1024,512]{2,1,0:T(8,128)} async-done(((f32[2,4096,512]{2,1,0:T(8,128)}), f32[2,1024,512]{2,1,0:T(8,128)}) %reduce-scatter.2.cloned.1.call-update) | async-done | bytes 4194320 | tf_op jit(solution)/shard_map/reduce_scatter | solution.py:92
  916.5 5.4 copy.82
  921.9 98.4 %all_to_all.30 = f32[2,1024,512]{2,0,1:T(2,128)S(1)} all-to-all(f32[2,1024,512]{2,0,1:T(2,128)S(1)} %copy.82), channel_id=1, replica_groups=mesh['depth'=4,'tile'=8] {'tile'}, dimensions={1} | all-to-all | bytes 8388608 | tf_op jit(solution)/shard_map/all_to_all | solution.py:93
  1020.3 2.7 copy.83
  1023.0 5.4 copy.84
  1028.4 8.3 fusion.41
  1036.7 1.4 multiply_subtract_fusion.3
  1038.1 0.6 pad_maximum_fusion.3
  1038.7 4.8 fusion.44
  1043.5 1.2 copy.88
  1044.8 1.8 copy.89
  (2 shorter events, 0.0 us)
Async XLA Ops:
  140.5 370.2 %all-to-all-start = ((f32[2,4096,512]{2,0,1:T(2,128)}), f32[2,4096,512]{2,0,1:T(2,128)}, u32[]{:S(2)}, u32[]{:S(2)}) async-start(f32[2,4096,512]{2,0,1:T(2,128)} %copy.67), calls=%async_computation | async-start | bytes 33554432 | tf_op jit(solution)/shard_map/all_to_all | solution.py:82
  146.8 769.6 %reduce-scatter.2.cloned.1.call-start = ((), (), s32[]{:S(2)}) async-start(), calls=%async_computation.3 | async-start | bytes 20971520 | tf_op jit(solution)/shard_map/reduce_scatter | solution.py:92
  663.6 8.4 copy-start
Sparse Core Ops, SparseCore 0:
  763.2 153.2 reduce-scatter.1
where the time goes:
time: 1060 us; the launch traced here: 1050 us
  waiting for transfers between devices  505 us (48%)
  matrix products  189 us (18%)
  local copies, waits for them, and re-layouts  162 us (15%)
  blocking collectives  98.4 us (9%)
  other arithmetic  78.9 us (7%)
  between operations  13.7 us (1%)
    all_to_all x1, waiting for transfers between devices, body(): lax.all_to_all(row_spec, 'tile', split_axis=1, concat_axis=2, tiled=True)  352 us
    dot_general x8, matrix products, contract(): jnp.einsum(form, values, matrix, precision=lax.Precision.HIGHEST, preferr...  189 us
    reduce_scatter x1, waiting for transfers between devices, body(): lax.psum_scatter(back_cols, 'depth', scatter_dimension=1, tiled=True)  153 us
    all_to_all x1, blocking collectives, body(): lax.all_to_all(partial_rows, 'tile', split_axis=1, concat_axis=2, tiled=T...  98.4 us
    dot_general x2, local copies, waits for them, and re-layouts, contract(): jnp.einsum(form, values, matrix, precision=lax.Precision.HIGHEST, preferr...  33 us
    reshape x1, local copies, waits for them, and re-layouts, transform(): return contract(form_full, turned, inner_mat).reshape((2,) + shape_out)  32.2 us
    all_to_all x2, local copies, waits for them, and re-layouts, body(): lax.all_to_all(row_spec, 'tile', split_axis=1, concat_axis=2, tiled=True)  31.4 us
    another operation x4, other arithmetic, transform(): jnp.stack([middle[0] * twist_re - middle[1] * twist_im, middle[0] * twist...  25 us
  transfers between devices with their start and end apart: 2, of which 2 were waited for; matrix products, arithmetic and copies ran while one was open for 1% of the time, Pallas kernels for 0%

commit v1 on v0

v1 whole, which is shorter than its diff:
```python
import functools
import math

import jax
import jax.numpy as jnp
import ml_dtypes
import numpy as np
from jax import lax
from jax.experimental import pallas as pl
from jax.experimental.pallas import tpu as pltpu
from jax.sharding import PartitionSpec as P

CHUNKS = 4
STRIP = 16
BF16 = ml_dtypes.bfloat16
F32 = jnp.float32


def halves_np(table):
    table = table.astype(np.float32)
    high = table.astype(BF16)
    low = (table - high.astype(np.float32)).astype(BF16)
    return high, low


def halves(value):
    high = value.astype(jnp.bfloat16)
    return high, (value - high.astype(F32)).astype(jnp.bfloat16)


def angles(rows, cols, modulus):
    turn = (rows[:, None] * cols[None, :]) % modulus
    phase = 2.0 * np.pi * turn / modulus
    return np.cos(phase), np.sin(phase)


def row_matrix(length, groups):
    index = np.arange(length)
    cos, sin = angles(index, index, length)
    width = length // groups
    cos = cos.reshape(length, groups, width)
    sin = sin.reshape(length, groups, width)
    top = np.concatenate([cos, -sin], axis=2).reshape(length, 2 * length)
    bottom = np.concatenate([sin, cos], axis=2).reshape(length, 2 * length)
    return halves_np(np.concatenate([top, bottom], axis=0))


def col_matrix(length):
    index = np.arange(length)
    cos, sin = angles(index, index, length)
    return halves_np(np.block([[cos, sin], [-sin, cos]]))


def dot(left, right):
    return jnp.dot(left, right, preferred_element_type=F32)


def dot3(left_high, left_low, right_high, right_low):
    return dot(left_high, right_high) + (dot(left_high, right_low) + dot(left_low, right_high))


def short_dft(values, sign):
    count = len(values)
    if count == 1:
        return values
    even = short_dft(values[0::2], sign)
    odd = short_dft(values[1::2], sign)
    half = count // 2
    out = [None] * count
    for k in range(half):
        re, im = odd[k]
        if 8 * k == 2 * count:
            re, im = (-sign * im, sign * re)
        elif k:
            c = math.cos(2.0 * math.pi * k / count)
            s = sign * math.sin(2.0 * math.pi * k / count)
            re, im = (re * c - im * s, re * s + im * c)
        out[k] = (even[k][0] + re, even[k][1] + im)
        out[k + half] = (even[k][0] - re, even[k][1] - im)
    return out


def row_kernel(k, x_ref, tw_ref, wh_ref, wl_ref, out_ref, yh, yl):
    rows, full = x_ref.shape
    length = full // CHUNKS
    width = out_ref.shape[-1]

    @pl.when(pl.program_id(0) == 0)
    def _():
        @pl.loop(0, rows // STRIP)
        def _(i):
            at = pl.ds(pl.multiple_of(i * STRIP, STRIP), STRIP)
            for lo in range(0, length, 256):
                x = [x_ref[at, a * length + lo : a * length + lo + 256] for a in range(4)]
                here = slice(lo, lo + 256)
                if k == 0:
                    re = (x[0] + x[2]) + (x[1] + x[3])
                    yh[at, here], yl[at, here] = halves(re)
                else:
                    c, s = (tw_ref[0:1, here], tw_ref[1:2, here])
                    if k == 2:
                        base = (x[0] + x[2]) - (x[1] + x[3])
                        re, im = (base * c, -base * s)
                    else:
                        a, b = (x[0] - x[2], x[1] - x[3])
                        b = -b if k == 1 else b
                        re, im = (a * c + b * s, b * c - a * s)
                    yh[at, here], yl[at, here] = halves(re)
                    there = slice(length + lo, length + lo + 256)
                    yh[at, there], yl[at, there] = halves(im)

    res = dot3(yh[...], yl[...], wh_ref[...], wl_ref[...])
    group = res.shape[1] // 2
    for j in range(group // width):
        for s in range(2):
            out_ref[j, s] = res[:, s * group + j * width : s * group + (j + 1) * width]


def row_chunk(k, x, tw, wh, wl, tiles):
    rows, full = x.shape
    length = full // CHUNKS
    depth = length if k == 0 else 2 * length
    width = length // tiles
    groups, _, double = wh.shape
    part = tiles // groups
    return pl.pallas_call(
        functools.partial(row_kernel, k),
        out_shape=jax.ShapeDtypeStruct((tiles, 2, rows, width), F32),
        grid=(groups,),
        in_specs=[
            pl.BlockSpec((rows, full), lambda t: (0, 0)),
            pl.BlockSpec((2, length), lambda t: (0, 0)),
            pl.BlockSpec((None, depth, double), lambda t: (t, 0, 0)),
            pl.BlockSpec((None, depth, double), lambda t: (t, 0, 0)),
        ],
        out_specs=pl.BlockSpec((part, 2, rows, width), lambda t: (t, 0, 0, 0)),
        scratch_shapes=[pltpu.VMEM((rows, depth), jnp.bfloat16)] * 2,
        compiler_params=pltpu.CompilerParams(vmem_limit_bytes=50 * 2**20),
        cost_estimate=pl.CostEstimate(
            flops=12 * rows * depth * length, bytes_accessed=rows * full * 8, transcendentals=0
        ),
        name=f"row{k}",
    )(x, tw, wh, wl)


def col_kernel(d_ref, t_ref, tw_ref, mh_ref, ml_ref, out_ref, yh, yl, ph, plow, res_ref):
    tiles, _, rows, width = d_ref.shape
    pitch = yh.shape[1] // tiles
    block = out_ref.shape[2]

    @pl.loop(0, rows // STRIP)
    def _(i):
        at = pl.ds(pl.multiple_of(i * STRIP, STRIP), STRIP)
        below = pl.ds(pl.multiple_of(rows + i * STRIP, STRIP), STRIP)
        out = short_dft([(d_ref[a, 0, at, :], d_ref[a, 1, at, :]) for a in range(tiles)], -1.0)
        for kk in range(tiles):
            re, im = out[kk]
            if kk:
                c, s = (tw_ref[kk, 0, at, :], tw_ref[kk, 1, at, :])
                re, im = (re * c + im * s, im * c - re * s)
            lanes = slice(kk * pitch, kk * pitch + width)
            yh[at, lanes], yl[at, lanes] = halves(re)
            yh[below, lanes], yl[below, lanes] = halves(im)

    @pl.loop(0, tiles // 2)
    def _(g):
        lanes = pl.ds(pl.multiple_of(g * 2 * pitch, 2 * pitch), 2 * pitch)
        spec = dot3(mh_ref[...], ml_ref[...], yh[:, lanes], yl[:, lanes])
        for h in range(2):
            there = slice(h * pitch, h * pitch + width)
            re, im = (spec[:rows, there], spec[rows:, there])
            tr = t_ref[0, 2 * g + h].astype(F32)
            ti = t_ref[1, 2 * g + h].astype(F32)
            ph[:rows, there], plow[:rows, there] = halves(re * ti + im * tr)
            ph[rows:, there], plow[rows:, there] = halves(re * tr - im * ti)
        back = dot3(mh_ref[...], ml_ref[...], ph[...], plow[...])
        for h in range(2):
            res_ref[2 * g + h] = back[:, h * pitch : h * pitch + width]

    @pl.loop(0, rows // STRIP)
    def _(i):
        at = pl.ds(pl.multiple_of(i * STRIP, STRIP), STRIP)
        below = pl.ds(pl.multiple_of(rows + i * STRIP, STRIP), STRIP)
        parts = []
        for kk in range(tiles):
            re, im = (res_ref[kk, below, :], res_ref[kk, at, :])
            if kk:
                c, s = (tw_ref[kk, 0, at, :], tw_ref[kk, 1, at, :])
                re, im = (re * c - im * s, im * c + re * s)
            parts.append((re, im))
        out = short_dft(parts, 1.0)
        for a in range(tiles):
            for s in range(2):
                if block >= STRIP:
                    per = block // STRIP
                    spot = pl.ds(pl.multiple_of((i % per) * STRIP, STRIP), STRIP)
                    out_ref[a * (rows // block) + i // per, s, spot, :] = out[a][s]
                else:
                    per = STRIP // block
                    for b in range(per):
                        piece = out[a][s][b * block : (b + 1) * block]
                        out_ref[a * (rows // block) + i * per + b, s] = piece


def col_chunk(k, data, response, tw, mh, ml, block):
    tiles, _, rows, width = data.shape
    pitch = max(width, 128)
    vm = pl.BlockSpec(memory_space=pltpu.VMEM)
    return pl.pallas_call(
        col_kernel,
        out_shape=jax.ShapeDtypeStruct((tiles * rows // block, 2, block, width), F32),
        in_specs=[vm] * 5,
        out_specs=vm,
        scratch_shapes=[pltpu.VMEM((2 * rows, tiles * pitch), jnp.bfloat16)] * 2
        + [pltpu.VMEM((2 * rows, 2 * pitch), jnp.bfloat16)] * 2
        + [pltpu.VMEM((tiles, 2 * rows, width), F32)],
        compiler_params=pltpu.CompilerParams(vmem_limit_bytes=56 * 2**20),
        cost_estimate=pl.CostEstimate(
            flops=48 * rows * rows * tiles * width,
            bytes_accessed=tiles * rows * width * 24,
            transcendentals=0,
        ),
        name=f"col{k}",
    )(data, response, tw, mh, ml)


def last_kernel(k, e_ref, tw_ref, wh_ref, wl_ref, *rest):
    acc_ref = rest[0] if k else None
    out_ref, yh, yl = rest[-3:]
    tiles, _, rows, width = e_ref.shape
    length = tiles * width
    group = wh_ref.shape[-1] // 2

    @pl.when(pl.program_id(0) == 0)
    def _():
        for t in range(tiles):
            for s in range(2):
                lo = (1 - s) * length + t * width
                yh[:, lo : lo + width], yl[:, lo : lo + width] = halves(e_ref[t, s])

    res = dot3(yh[...], yl[...], wh_ref[...], wl_ref[...])
    im, re = (res[:, :group], res[:, group:])
    c, s = (tw_ref[0:1, :], tw_ref[1:2, :])
    if k == 0:
        real = re * c
        terms = [real] * 4
    else:
        real, imag = (re * c - im * s, re * s + im * c)
        turns = [real, -imag, -real, imag]
        terms = [turns[(k * a) % 4] for a in range(4)]
    for a in range(4):
        spot = pl.ds(pl.multiple_of(a * length + pl.program_id(0) * group, group), group)
        out_ref[:, spot] = terms[a] if k == 0 else acc_ref[:, spot] + terms[a]


def last_chunk(k, data, tw, wh, wl, acc):
    tiles, _, rows, width = data.shape
    length = tiles * width
    groups, _, double = wh.shape
    specs = [
        pl.BlockSpec((tiles, 2, rows, width), lambda t: (0, 0, 0, 0)),
        pl.BlockSpec((2, double // 2), lambda t: (0, t)),
        pl.BlockSpec((None, 2 * length, double), lambda t: (t, 0, 0)),
        pl.BlockSpec((None, 2 * length, double), lambda t: (t, 0, 0)),
    ]
    part = pl.BlockSpec((rows, 4 * length), lambda t: (0, 0))
    args = [data, tw, wh, wl]
    if k:
        specs.append(part)
        args.append(acc)
    return pl.pallas_call(
        functools.partial(last_kernel, k),
        out_shape=jax.ShapeDtypeStruct((rows, 4 * length), F32),
        grid=(groups,),
        in_specs=specs,
        out_specs=part,
        scratch_shapes=[pltpu.VMEM((rows, 2 * length), jnp.bfloat16)] * 2,
        compiler_params=pltpu.CompilerParams(vmem_limit_bytes=40 * 2**20),
        cost_estimate=pl.CostEstimate(
            flops=24 * rows * length * length, bytes_accessed=2**24, transcendentals=0
        ),
        name=f"last{k}",
    )(*args)


def body(objects, transfer):
    tiles = lax.axis_size("tile")
    depths = lax.axis_size("depth")
    rows, full = objects.shape[1:]
    height = rows * tiles
    length = full // CHUNKS
    width = length // tiles
    block = height // (tiles * depths)
    group = max(width, 128)
    groups = length // group
    wh, wl = (
        jnp.asarray(
            np.ascontiguousarray(
                table.reshape(2 * length, groups, 2 * group).transpose(1, 0, 2)
            )
        )
        for table in row_matrix(length, groups)
    )
    mh, ml = (jnp.asarray(m) for m in col_matrix(rows))
    twist = np.stack(angles(np.arange(CHUNKS), np.arange(length), full), axis=1).astype(np.float32)
    final = jnp.asarray(twist / (height * full))
    twist = jnp.asarray(twist)
    turn = np.stack(angles(np.arange(tiles), np.arange(rows), height), axis=1).astype(np.float32)
    turn = jnp.broadcast_to(jnp.asarray(turn)[..., None], turn.shape + (width,))

    pick = np.zeros((CHUNKS * width, CHUNKS, width), np.float32)
    for k in range(CHUNKS):
        for m in range(width):
            pick[CHUNKS * m + k, k, m] = 1.0
    pick = jnp.asarray(pick.astype(BF16))
    split = transfer[0].reshape(2, rows, tiles, CHUNKS * width)
    response = [
        jnp.einsum("smkl,lw->skmw", split, pick[:, k], preferred_element_type=F32).astype(
            jnp.bfloat16
        )
        for k in range(CHUNKS)
    ]

    x = objects[0]
    sent = [row_chunk(k, x, twist[k], wh, wl, tiles) for k in range(CHUNKS)]
    acc = None
    for k in range(CHUNKS):
        bands = lax.all_to_all(sent[k], "tile", split_axis=0, concat_axis=0, tiled=True)
        back = col_chunk(k, bands, response[k], turn, mh, ml, block)
        summed = lax.psum_scatter(back, "depth", scatter_dimension=0, tiled=True)
        owned = lax.all_to_all(summed, "tile", split_axis=0, concat_axis=0, tiled=True)
        acc = last_chunk(k, owned, final[k], wh, wl, acc)
    return acc


def solution(mesh):
    in_specs = (P("depth", "tile", None), P("depth", None, None, "tile"))
    out_specs = P(("depth", "tile"), None)
    return jax.shard_map(body, mesh=mesh, in_specs=in_specs, out_specs=out_specs, check_vma=False)
```

time: 1060 us -> 608 us (0.57)
  waiting for transfers between devices: 505 us -> 234 us
  Pallas kernels: 0 us -> 265 us
  matrix products: 189 us -> 38.7 us
  local copies, waits for them, and re-layouts: 162 us -> 12.7 us
  blocking collectives: 98.4 us -> 0 us
  other arithmetic: 78.9 us -> 0 us
  starting transfers between devices: 6.39 us -> 36.3 us
    pallas_call x0 -> x12, Pallas kernels: none -> 265 us  [the longest x4 153 us: col_chunk(): pl.pallas_call(col_kernel, out_shape=jax.ShapeDtypeStruct((tiles * rows /...]
    reduce_scatter x1 -> x4, waiting for transfers between devices: 153 us -> 0.08 us  [body(): summed = lax.psum_scatter(back, 'depth', scatter_dimension=0, tiled=True)]
    dot_general x8 -> x4, matrix products: 189 us -> 38.7 us  [body(): jnp.einsum('smkl,lw->skmw', split, pick[:, k], preferred_element_type=F32)]
    all_to_all x1 -> x8, waiting for transfers between devices: 352 us -> 233 us  [the longest x4 154 us: body(): lax.all_to_all(sent[k], 'tile', split_axis=0, concat_axis=0, tiled=True)]
    all_to_all x1 -> x0, blocking collectives: 98.4 us -> none  [body(): lax.all_to_all(partial_rows, 'tile', split_axis=1, concat_axis=2, tiled=T...]
    sub x5 -> x0, other arithmetic: 41.4 us -> none  [the longest x4 22 us: transform(): middle[0] * twist_re - middle[1] * twist_im]
    all_to_all x4 -> x0, local copies, waits for them, and re-layouts: 39.5 us -> none  [the longest x2 31.4 us: body(): lax.all_to_all(row_spec, 'tile', split_axis=1, concat_axis=2, tiled=True)]
    dot_general x2 -> x0, local copies, waits for them, and re-layouts: 33 us -> none  [contract(): jnp.einsum(form, values, matrix, precision=lax.Precision.HIGHEST, preferr...]
  transfers between devices with their start and end apart: 2 -> 12, of which waited for: 2 -> 7; matrix products, arithmetic and copies ran while one was open for 1% -> 7% of each run, Pallas kernels for 0% -> 40%
where the time goes in v1:
time: 608 us; the launch traced here: 600 us
  Pallas kernels  265 us (44%)
  waiting for transfers between devices  234 us (38%)
  matrix products  38.7 us (6%)
  starting transfers between devices  36.3 us (6%)
  between operations  13.5 us (2%)
  local copies, waits for them, and re-layouts  12.7 us (2%)
    all_to_all x4, waiting for transfers between devices, body(): lax.all_to_all(sent[k], 'tile', split_axis=0, concat_axis=0, tiled=True)  154 us
    pallas_call x4, Pallas kernels, col_chunk(): pl.pallas_call(col_kernel, out_shape=jax.ShapeDtypeStruct((tiles * rows /...  153 us
    all_to_all x4, waiting for transfers between devices, body(): lax.all_to_all(summed, 'tile', split_axis=0, concat_axis=0, tiled=True)  79.4 us
    pallas_call x4, Pallas kernels, row_chunk(): pl.pallas_call(functools.partial(row_kernel, k), out_shape=jax.ShapeDtype...  76.6 us
    dot_general x4, matrix products, body(): jnp.einsum('smkl,lw->skmw', split, pick[:, k], preferred_element_type=F32)  38.7 us
    pallas_call x4, Pallas kernels, last_chunk(): pl.pallas_call(functools.partial(last_kernel, k), out_shape=jax.ShapeDtyp...  35.6 us
    all_to_all x4, starting transfers between devices, body(): lax.all_to_all(sent[k], 'tile', split_axis=0, concat_axis=0, tiled=True)  20.2 us
    all_to_all x4, starting transfers between devices, body(): lax.all_to_all(summed, 'tile', split_axis=0, concat_axis=0, tiled=True)  15.1 us
  transfers between devices with their start and end apart: 12, of which 7 were waited for; matrix products, arithmetic and copies ran while one was open for 7% of the time, Pallas kernels for 40%

profile of v1, /device:TPU:0, one launch (start us, length us, event | category | flops | bytes accessed | tf_op | source)
XLA Modules:
  0.0 600.3 jit_solution(10759700792568902178)
XLA Ops:
  6.5 0.7 copy-done.6
  7.2 14.6 %row0.1 = f32[8,2,512,128]{3,2,1,0:T(8,128)} custom-call(f32[512,4096]{1,0:T(8,128)} %bitcast.26, f32[2,1024]{1,0:T(2,128)S(1)} %copy-done.6, bf16[8,2048,256]{2,1,0:T(8,128)(2,1)} %constant.16.clone.wh_ref, bf16[8,2048,256]{2,1,0:T(8,128)(2,1)} %constant.17.clone.wl_ref), custom_call_target="tpu_custom_call" | custom-call | flops 6442450944 | bytes 16777216 | tf_op jit(solution)/shard_map/row0/pallas_call | solution.py:126
  21.8 6.5 %all-to-all-start.6 = ((f32[8,2,512,128]{3,2,1,0:T(8,128)}), f32[8,2,512,128]{3,2,1,0:T(8,128)}, u32[]{:S(2)}, u32[]{:S(2)}) async-start(f32[8,2,512,128]{3,2,1,0:T(8,128)} %row0.1), calls=%async_computation.9 | async-start | bytes 8388608 | tf_op jit(solution)/shard_map/all_to_all | solution.py:328
  28.3 0.0 copy-done.14
  28.3 0.0 copy-start.9
  28.3 9.7 %convert_bitcast_fusion.t_ref = bf16[2,8,512,128]{3,2,1,0:T(8,128)(2,1)} fusion(bf16[512,128,1,1]{0,1,3,2:T(8,128)(2,1)S(1)} %copy-done.14, bf16[2,512,8,512]{3,2,1,0:T(8,128)(2,1)} %bitcast.30), kind=kOutput, calls=%fused_computation.8 | convolution fusion | flops 1074790400 | bytes 10616832 | tf_op jit(solution)/shard_map/smkl,lw->skmw/dot_general | solution.py:318
  38.0 0.0 copy-done.9
  38.0 20.7 %row1.1 = f32[8,2,512,128]{3,2,1,0:T(8,128)} custom-call(f32[512,4096]{1,0:T(8,128)} %bitcast.27, f32[2,1024]{1,0:T(2,128)S(1)} %copy-done.9, bf16[8,2048,256]{2,1,0:T(8,128)(2,1)} %constant.16.clone.wh_ref, bf16[8,2048,256]{2,1,0:T(8,128)(2,1)} %constant.17.clone.wl_ref), custom_call_target="tpu_custom_call" | custom-call | flops 12884901888 | bytes 16777216 | tf_op jit(solution)/shard_map/row1/pallas_call | solution.py:126
  58.7 63.7 %all-to-all-done.6.d_ref = f32[8,2,512,128]{3,2,1,0:T(8,128)} async-done(((f32[8,2,512,128]{3,2,1,0:T(8,128)}), f32[8,2,512,128]{3,2,1,0:T(8,128)}, u32[]{:S(2)}, u32[]{:S(2)}) %all-to-all-start.6) | async-done | bytes 4194336 | tf_op jit(solution)/shard_map/all_to_all | solution.py:328
  122.4 4.6 all-to-all-start.4
  127.0 0.2 reduce-scatter.11.cloned.1.call-start
  127.2 0.0 copy-done.10
  127.2 2.6 broadcast_in_dim.2.tw_ref
  129.9 38.3 %col0.1 = f32[32,2,128,128]{3,2,1,0:T(8,128)} custom-call(f32[8,2,512,128]{3,2,1,0:T(8,128)} %all-to-all-done.6.d_ref, bf16[2,8,512,128]{3,2,1,0:T(8,128)(2,1)} %convert_bitcast_fusion.t_ref, f32[8,2,512,128]{3,2,1,0:T(8,128)} %broadcast_in_dim.2.tw_ref, bf16[1024,1024]{1,0:T(8,128)(2,1)} %constant.18.clone.mh_ref, bf16[1024,1024]{1,0:T(8,128)(2,1)} %constant.19.clone.ml_ref), custom_call_target="tpu_custom_call" | custom-call | flops 12884901888 | bytes 12582912 | tf_op jit(solution)/shard_map/col0/pallas_call | solution.py:209
  168.2 0.0 reduce-scatter.11.cloned.1.call-update
  168.2 0.9 copy-done.13
  169.1 9.7 %convert_bitcast_fusion.1.t_ref = bf16[2,8,512,128]{3,2,1,0:T(8,128)(2,1)} fusion(bf16[512,128,1,1]{0,1,3,2:T(8,128)(2,1)S(1)} %copy-done.13, bf16[2,512,8,512]{3,2,1,0:T(8,128)(2,1)} %bitcast.31), kind=kOutput, calls=%fused_computation.9 | convolution fusion | flops 1074790400 | bytes 10616832 | tf_op jit(solution)/shard_map/smkl,lw->skmw/dot_general | solution.py:318
  178.8 0.0 copy-done.8
  178.8 20.6 %row2.1 = f32[8,2,512,128]{3,2,1,0:T(8,128)} custom-call(f32[512,4096]{1,0:T(8,128)} %bitcast.28, f32[2,1024]{1,0:T(2,128)S(1)} %copy-done.8, bf16[8,2048,256]{2,1,0:T(8,128)(2,1)} %constant.16.clone.wh_ref, bf16[8,2048,256]{2,1,0:T(8,128)(2,1)} %constant.17.clone.wl_ref), custom_call_target="tpu_custom_call" | custom-call | flops 12884901888 | bytes 16777216 | tf_op jit(solution)/shard_map/row2/pallas_call | solution.py:126
  199.4 21.6 %all-to-all-done.4.d_ref = f32[8,2,512,128]{3,2,1,0:T(8,128)} async-done(((f32[8,2,512,128]{3,2,1,0:T(8,128)}), f32[8,2,512,128]{3,2,1,0:T(8,128)}, u32[]{:S(2)}, u32[]{:S(2)}) %all-to-all-start.4) | async-done | bytes 4194336 | tf_op jit(solution)/shard_map/all_to_all | solution.py:328
  221.0 4.6 all-to-all-start.2
  225.6 0.3 reduce-scatter.9.cloned.1.call-start
  225.8 38.3 %col1.1 = f32[32,2,128,128]{3,2,1,0:T(8,128)} custom-call(f32[8,2,512,128]{3,2,1,0:T(8,128)} %all-to-all-done.4.d_ref, bf16[2,8,512,128]{3,2,1,0:T(8,128)(2,1)} %convert_bitcast_fusion.1.t_ref, f32[8,2,512,128]{3,2,1,0:T(8,128)} %broadcast_in_dim.2.tw_ref, bf16[1024,1024]{1,0:T(8,128)(2,1)} %constant.18.clone.mh_ref, bf16[1024,1024]{1,0:T(8,128)(2,1)} %constant.19.clone.ml_ref), custom_call_target="tpu_custom_call" | custom-call | flops 12884901888 | bytes 12582912 | tf_op jit(solution)/shard_map/col1/pallas_call | solution.py:209
  264.1 0.0 reduce-scatter.9.cloned.1.call-update
  264.2 0.9 copy-done.12
  265.0 9.7 %convert_bitcast_fusion.2.t_ref = bf16[2,8,512,128]{3,2,1,0:T(8,128)(2,1)} fusion(bf16[512,128,1,1]{0,1,3,2:T(8,128)(2,1)S(1)} %copy-done.12, bf16[2,512,8,512]{3,2,1,0:T(8,128)(2,1)} %bitcast.32), kind=kOutput, calls=%fused_computation.10 | convolution fusion | flops 1074790400 | bytes 10616832 | tf_op jit(solution)/shard_map/smkl,lw->skmw/dot_general | solution.py:318
  274.7 0.0 copy-done.7
  274.7 20.7 %row3.1 = f32[8,2,512,128]{3,2,1,0:T(8,128)} custom-call(f32[512,4096]{1,0:T(8,128)} %bitcast.29, f32[2,1024]{1,0:T(2,128)S(1)} %copy-done.7, bf16[8,2048,256]{2,1,0:T(8,128)(2,1)} %constant.16.clone.wh_ref, bf16[8,2048,256]{2,1,0:T(8,128)(2,1)} %constant.17.clone.wl_ref), custom_call_target="tpu_custom_call" | custom-call | flops 12884901888 | bytes 16777216 | tf_op jit(solution)/shard_map/row3/pallas_call | solution.py:126
  295.4 24.1 %all-to-all-done.2.d_ref = f32[8,2,512,128]{3,2,1,0:T(8,128)} async-done(((f32[8,2,512,128]{3,2,1,0:T(8,128)}), f32[8,2,512,128]{3,2,1,0:T(8,128)}, u32[]{:S(2)}, u32[]{:S(2)}) %all-to-all-start.2) | async-done | bytes 4194336 | tf_op jit(solution)/shard_map/all_to_all | solution.py:328
  319.5 4.6 all-to-all-start
  324.1 0.4 reduce-scatter.7.cloned.1.call-start
  324.6 38.3 %col2.1 = f32[32,2,128,128]{3,2,1,0:T(8,128)} custom-call(f32[8,2,512,128]{3,2,1,0:T(8,128)} %all-to-all-done.2.d_ref, bf16[2,8,512,128]{3,2,1,0:T(8,128)(2,1)} %convert_bitcast_fusion.2.t_ref, f32[8,2,512,128]{3,2,1,0:T(8,128)} %broadcast_in_dim.2.tw_ref, bf16[1024,1024]{1,0:T(8,128)(2,1)} %constant.18.clone.mh_ref, bf16[1024,1024]{1,0:T(8,128)(2,1)} %constant.19.clone.ml_ref), custom_call_target="tpu_custom_call" | custom-call | flops 12884901888 | bytes 12582912 | tf_op jit(solution)/shard_map/col2/pallas_call | solution.py:209
  362.8 0.0 reduce-scatter.7.cloned.1.call-update
  362.9 0.0 reduce-scatter.5.cloned.1.call-start
  362.9 0.8 copy-done.11
  363.7 9.7 %convert_bitcast_fusion.3.t_ref = bf16[2,8,512,128]{3,2,1,0:T(8,128)(2,1)} fusion(bf16[512,128,1,1]{0,1,3,2:T(8,128)(2,1)S(1)} %copy-done.11, bf16[2,512,8,512]{3,2,1,0:T(8,128)(2,1)} %bitcast.33), kind=kOutput, calls=%fused_computation.11 | convolution fusion | flops 1074790400 | bytes 10616832 | tf_op jit(solution)/shard_map/smkl,lw->skmw/dot_general | solution.py:318
  373.4 44.7 %all-to-all-done.d_ref = f32[8,2,512,128]{3,2,1,0:T(8,128)} async-done(((f32[8,2,512,128]{3,2,1,0:T(8,128)}), f32[8,2,512,128]{3,2,1,0:T(8,128)}, u32[]{:S(2)}, u32[]{:S(2)}) %all-to-all-start) | async-done | bytes 4194336 | tf_op jit(solution)/shard_map/all_to_all | solution.py:328
  418.1 38.4 %col3.1 = f32[32,2,128,128]{3,2,1,0:T(8,128)} custom-call(f32[8,2,512,128]{3,2,1,0:T(8,128)} %all-to-all-done.d_ref, bf16[2,8,512,128]{3,2,1,0:T(8,128)(2,1)} %convert_bitcast_fusion.3.t_ref, f32[8,2,512,128]{3,2,1,0:T(8,128)} %broadcast_in_dim.2.tw_ref, bf16[1024,1024]{1,0:T(8,128)(2,1)} %constant.18.clone.mh_ref, bf16[1024,1024]{1,0:T(8,128)(2,1)} %constant.19.clone.ml_ref), custom_call_target="tpu_custom_call" | custom-call | flops 12884901888 | bytes 12582912 | tf_op jit(solution)/shard_map/col3/pallas_call | solution.py:209
  456.5 0.0 reduce-scatter.5.cloned.1.call-update
  456.5 0.0 copy-start.5
  456.5 0.0 reduce-scatter.11.cloned.1.call-done
  456.5 3.6 all-to-all-start.7
  460.1 0.0 reduce-scatter.9.cloned.1.call-done
  460.1 26.5 %all-to-all-done.7.e_ref = f32[8,2,128,128]{3,2,1,0:T(8,128)S(1)} async-done(((f32[8,2,128,128]{3,2,1,0:T(8,128)}), f32[8,2,128,128]{3,2,1,0:T(8,128)S(1)}, u32[]{:S(2)}, u32[]{:S(2)}) %all-to-all-start.7) | async-done | bytes 1048608 | tf_op jit(solution)/shard_map/all_to_all | solution.py:331
  486.6 3.6 all-to-all-start.5
  490.2 0.0 reduce-scatter.7.cloned.1.call-done
  490.2 26.5 %all-to-all-done.5.e_ref = f32[8,2,128,128]{3,2,1,0:T(8,128)S(1)} async-done(((f32[8,2,128,128]{3,2,1,0:T(8,128)}), f32[8,2,128,128]{3,2,1,0:T(8,128)S(1)}, u32[]{:S(2)}, u32[]{:S(2)}) %all-to-all-start.5) | async-done | bytes 1048608 | tf_op jit(solution)/shard_map/all_to_all | solution.py:331
  516.7 3.6 all-to-all-start.3
  520.2 0.0 reduce-scatter.5.cloned.1.call-done
  520.3 26.5 %all-to-all-done.3.e_ref = f32[8,2,128,128]{3,2,1,0:T(8,128)S(1)} async-done(((f32[8,2,128,128]{3,2,1,0:T(8,128)}), f32[8,2,128,128]{3,2,1,0:T(8,128)S(1)}, u32[]{:S(2)}, u32[]{:S(2)}) %all-to-all-start.3) | async-done | bytes 1048608 | tf_op jit(solution)/shard_map/all_to_all | solution.py:331
  546.7 4.4 all-to-all-start.1
  551.1 0.0 copy-start
  551.2 3.4 copy-done
  554.5 8.5 %last0.1.rest_0_ = f32[128,4096]{1,0:T(8,128)S(1)} custom-call(f32[8,2,128,128]{3,2,1,0:T(8,128)S(1)} %all-to-all-done.7.e_ref, f32[2,1024]{1,0:T(2,128)S(1)} %copy-done.5, bf16[8,2048,256]{2,1,0:T(8,128)(2,1)S(1)} %copy-done, bf16[8,2048,256]{2,1,0:T(8,128)(2,1)} %constant.17.clone.wl_ref), custom_call_target="tpu_custom_call" | custom-call | flops 3221225472 | bytes 16777216 | tf_op jit(solution)/shard_map/last0/pallas_call | solution.py:271
  563.0 0.0 copy-done.4
  563.0 0.0 copy-start.3
  563.0 8.5 %last1.1.rest_0_ = f32[128,4096]{1,0:T(8,128)S(1)} custom-call(f32[8,2,128,128]{3,2,1,0:T(8,128)S(1)} %all-to-all-done.5.e_ref, f32[2,1024]{1,0:T(2,128)S(1)} %copy-done.4, bf16[8,2048,256]{2,1,0:T(8,128)(2,1)S(1)} %copy-done, bf16[8,2048,256]{2,1,0:T(8,128)(2,1)} %constant.17.clone.wl_ref, f32[128,4096]{1,0:T(8,128)S(1)} %last0.1.rest_0_), custom_call_target="tpu_custom_call" | custom-call | flops 3221225472 | bytes 16777216 | tf_op jit(solution)/shard_map/last1/pallas_call | solution.py:271
  571.6 0.0 copy-done.3
  571.6 0.0 copy-start.2
  571.6 8.5 %last2.1.rest_0_ = f32[128,4096]{1,0:T(8,128)S(1)} custom-call(f32[8,2,128,128]{3,2,1,0:T(8,128)S(1)} %all-to-all-done.3.e_ref, f32[2,1024]{1,0:T(2,128)S(1)} %copy-done.3, bf16[8,2048,256]{2,1,0:T(8,128)(2,1)S(1)} %copy-done, bf16[8,2048,256]{2,1,0:T(8,128)(2,1)} %constant.17.clone.wl_ref, f32[128,4096]{1,0:T(8,128)S(1)} %last1.1.rest_0_), custom_call_target="tpu_custom_call" | custom-call | flops 3221225472 | bytes 16777216 | tf_op jit(solution)/shard_map/last2/pallas_call | solution.py:271
  580.1 0.0 all-to-all-done.1.e_ref
  580.1 0.0 copy-start.1
  580.1 3.4 copy-done.1
  583.5 10.1 %last3.1 = f32[128,4096]{1,0:T(8,128)} custom-call(f32[8,2,128,128]{3,2,1,0:T(8,128)} %all-to-all-done.1.e_ref, f32[2,1024]{1,0:T(2,128)S(1)} %copy-done.2, bf16[8,2048,256]{2,1,0:T(8,128)(2,1)S(1)} %copy-done.1, bf16[8,2048,256]{2,1,0:T(8,128)(2,1)} %constant.17.clone.wl_ref, f32[128,4096]{1,0:T(8,128)S(1)} %last2.1.rest_0_), custom_call_target="tpu_custom_call" | custom-call | flops 3221225472 | bytes 16777216 | tf_op jit(solution)/shard_map/last3/pallas_call | solution.py:271
  (11 shorter events, 0.0 us)
Async XLA Ops:
  6.5 0.7 copy-start.6
  21.8 6.5 %copy-start.14 = (bf16[512,128,1,1]{0,1,3,2:T(8,128)(2,1)S(1)}, bf16[512,128,1,1]{0,1,3,2:T(8,128)(2,1)}, u32[]{:S(2)}) copy-start(bf16[512,128,1,1]{0,1,3,2:T(8,128)(2,1)} %constant.53) | copy-start | bytes 393220
  21.8 100.6 %all-to-all-start.6 = ((f32[8,2,512,128]{3,2,1,0:T(8,128)}), f32[8,2,512,128]{3,2,1,0:T(8,128)}, u32[]{:S(2)}, u32[]{:S(2)}) async-start(f32[8,2,512,128]{3,2,1,0:T(8,128)} %row0.1), calls=%async_computation.9 | async-start | bytes 8388608 | tf_op jit(solution)/shard_map/all_to_all | solution.py:328
  28.3 9.7 %copy-start.9 = (f32[2,1024]{1,0:T(2,128)S(1)}, f32[2,1024]{1,0:T(2,128)}, u32[]{:S(2)}) copy-start(f32[2,1024]{1,0:T(2,128)} %constant.39.tw_ref) | copy-start | bytes 24580
  58.7 68.6 %copy-start.10 = (f32[8,2,512]{2,1,0:T(2,128)S(1)}, f32[8,2,512]{2,1,0:T(2,128)}, u32[]{:S(2)}) copy-start(f32[8,2,512]{2,1,0:T(2,128)} %constant.22.clone) | copy-start | bytes 98308
  122.4 98.6 %all-to-all-start.4 = ((f32[8,2,512,128]{3,2,1,0:T(8,128)}), f32[8,2,512,128]{3,2,1,0:T(8,128)}, u32[]{:S(2)}, u32[]{:S(2)}) async-start(f32[8,2,512,128]{3,2,1,0:T(8,128)} %row1.1), calls=%async_computation.6 | async-start | bytes 8388608 | tf_op jit(solution)/shard_map/all_to_all | solution.py:328
  127.0 329.5 %reduce-scatter.11.cloned.1.call-start = ((), (), s32[]{:S(2)}) async-start(), calls=%async_computation.15 | async-start | bytes 5242880 | tf_op jit(solution)/shard_map/reduce_scatter | solution.py:330
  168.2 0.9 copy-start.13
  169.1 9.7 %copy-start.8 = (f32[2,1024]{1,0:T(2,128)S(1)}, f32[2,1024]{1,0:T(2,128)}, u32[]{:S(2)}) copy-start(f32[2,1024]{1,0:T(2,128)} %constant.33.tw_ref) | copy-start | bytes 24580
  221.0 98.5 %all-to-all-start.2 = ((f32[8,2,512,128]{3,2,1,0:T(8,128)}), f32[8,2,512,128]{3,2,1,0:T(8,128)}, u32[]{:S(2)}, u32[]{:S(2)}) async-start(f32[8,2,512,128]{3,2,1,0:T(8,128)} %row2.1), calls=%async_computation.3 | async-start | bytes 8388608 | tf_op jit(solution)/shard_map/all_to_all | solution.py:328
  225.6 234.6 %reduce-scatter.9.cloned.1.call-start = ((), (), s32[]{:S(2)}) async-start(), calls=%async_computation.14 | async-start | bytes 5242880 | tf_op jit(solution)/shard_map/reduce_scatter | solution.py:330
  264.1 0.9 copy-start.12
  265.0 9.7 %copy-start.7 = (f32[2,1024]{1,0:T(2,128)S(1)}, f32[2,1024]{1,0:T(2,128)}, u32[]{:S(2)}) copy-start(f32[2,1024]{1,0:T(2,128)} %constant.27.tw_ref) | copy-start | bytes 24580
  319.5 98.6 %all-to-all-start = ((f32[8,2,512,128]{3,2,1,0:T(8,128)}), f32[8,2,512,128]{3,2,1,0:T(8,128)}, u32[]{:S(2)}, u32[]{:S(2)}) async-start(f32[8,2,512,128]{3,2,1,0:T(8,128)} %row3.1), calls=%async_computation | async-start | bytes 8388608 | tf_op jit(solution)/shard_map/all_to_all | solution.py:328
  324.1 166.1 %reduce-scatter.7.cloned.1.call-start = ((), (), s32[]{:S(2)}) async-start(), calls=%async_computation.13 | async-start | bytes 5242880 | tf_op jit(solution)/shard_map/reduce_scatter | solution.py:330
  362.8 0.9 copy-start.11
  362.9 157.4 %reduce-scatter.5.cloned.1.call-start = ((), (), s32[]{:S(2)}) async-start(), calls=%async_computation.12 | async-start | bytes 5242880 | tf_op jit(solution)/shard_map/reduce_scatter | solution.py:330
  456.5 94.6 %copy-start.5 = (f32[2,1024]{1,0:T(2,128)S(1)}, f32[2,1024]{1,0:T(2,128)}, u32[]{:S(2)}) copy-start(f32[2,1024]{1,0:T(2,128)} %constant.49.tw_ref) | copy-start | bytes 24580
  456.5 30.1 %all-to-all-start.7 = ((f32[8,2,128,128]{3,2,1,0:T(8,128)}), f32[8,2,128,128]{3,2,1,0:T(8,128)S(1)}, u32[]{:S(2)}, u32[]{:S(2)}) async-start(f32[8,2,128,128]{3,2,1,0:T(8,128)} %reduce-scatter.11.cloned.1.call-done), calls=%async_computation.11 | async-start | bytes 2097152 | tf_op jit(solution)/shard_map/all_to_all | solution.py:331
  486.6 30.1 %all-to-all-start.5 = ((f32[8,2,128,128]{3,2,1,0:T(8,128)}), f32[8,2,128,128]{3,2,1,0:T(8,128)S(1)}, u32[]{:S(2)}, u32[]{:S(2)}) async-start(f32[8,2,128,128]{3,2,1,0:T(8,128)} %reduce-scatter.9.cloned.1.call-done), calls=%async_computation.8 | async-start | bytes 2097152 | tf_op jit(solution)/shard_map/all_to_all | solution.py:331
  516.7 30.1 %all-to-all-start.3 = ((f32[8,2,128,128]{3,2,1,0:T(8,128)}), f32[8,2,128,128]{3,2,1,0:T(8,128)S(1)}, u32[]{:S(2)}, u32[]{:S(2)}) async-start(f32[8,2,128,128]{3,2,1,0:T(8,128)} %reduce-scatter.7.cloned.1.call-done), calls=%async_computation.5 | async-start | bytes 2097152 | tf_op jit(solution)/shard_map/all_to_all | solution.py:331
  546.7 33.4 %all-to-all-start.1 = ((f32[8,2,128,128]{3,2,1,0:T(8,128)}), f32[8,2,128,128]{3,2,1,0:T(8,128)}, u32[]{:S(2)}, u32[]{:S(2)}) async-start(f32[8,2,128,128]{3,2,1,0:T(8,128)} %reduce-scatter.5.cloned.1.call-done), calls=%async_computation.2 | async-start | bytes 2097152 | tf_op jit(solution)/shard_map/all_to_all | solution.py:331
  551.1 3.4 copy-start
  554.5 8.5 %copy-start.4 = (f32[2,1024]{1,0:T(2,128)S(1)}, f32[2,1024]{1,0:T(2,128)}, u32[]{:S(2)}) copy-start(f32[2,1024]{1,0:T(2,128)} %constant.43.tw_ref) | copy-start | bytes 24580
  563.0 8.5 %copy-start.3 = (f32[2,1024]{1,0:T(2,128)S(1)}, f32[2,1024]{1,0:T(2,128)}, u32[]{:S(2)}) copy-start(f32[2,1024]{1,0:T(2,128)} %constant.37.tw_ref) | copy-start | bytes 24580
  571.6 8.5 %copy-start.2 = (f32[2,1024]{1,0:T(2,128)S(1)}, f32[2,1024]{1,0:T(2,128)}, u32[]{:S(2)}) copy-start(f32[2,1024]{1,0:T(2,128)} %constant.31.tw_ref) | copy-start | bytes 24580
  580.1 3.4 copy-start.1
Sparse Core Ops, SparseCore 0:
  168.3 53.9 reduce-scatter.10
  264.3 53.9 reduce-scatter.8
  363.0 53.9 reduce-scatter.6
  456.6 51.5 reduce-scatter.4
